TPU v7x, 32 devices: a whole 2x2x4 slice. The times are simulated.
32 devices in a mesh: dom: 4 (over y, x), fsdp: 8 (over z, core).
Axes of the slice: x: 2, y: 2, z: 4, core: 2. Of those that a mesh axis runs over, the one named last changes fastest.
Arguments:
- inputs: bfloat16 [4, 1024, 4096], P('dom', 'fsdp'), may hold values from -6 to 6
- cotangent: bfloat16 [4, 1024, 8192], P('dom', 'fsdp'), may hold values from -6 to 6
- shared_weight: bfloat16 [4096, 8192], P(None, 'fsdp'), may hold values from -0.09375 to 0.09375
- domain_weight: bfloat16 [4, 4096, 8192], P('dom', None, 'fsdp'), may hold values from 0.099609375 to 1.8984375
- row_counts: int32 [4], P('dom'), may hold values from 65 to 1024, as said below
Outputs:
- shared_grad: float32 [4096, 8192], P('dom', 'fsdp')
- domain_grad: bfloat16 [4, 4096, 8192], P('dom', None, 'fsdp')
- input_grad: bfloat16 [4, 1024, 4096], P('dom', 'fsdp')
Inputs may be any that keep to these rules, and one draw needn't show every extreme that they name: `row_counts`: rows of a domain at positions from its count on are padding. Some domain is full in every draw.
All inputs are finite; a program needn't handle non-finite values.
Results may differ from a plain program's by a relative error of at most 0.017.
Values may be sent and summed in bfloat16 or wider, within the bound.
A program may use at most 128 MiB of HBM per device.

v0:
```python
import functools

import jax
import jax.numpy as jnp
from jax import lax
from jax.experimental import pallas as pl
from jax.experimental.pallas import tpu as pltpu
from jax.sharding import PartitionSpec as P

MESH = pl.DeviceIdType.MESH
F32 = jnp.float32
BF16 = jnp.bfloat16


def entry_barrier(axis, me, n):
    barrier = pltpu.get_barrier_semaphore()

    def greet(k, carry):
        pl.semaphore_signal(
            barrier, inc=1, device_id={axis: lax.rem(me + k, n)}, device_id_type=MESH
        )
        return carry

    lax.fori_loop(1, n, greet, 0)
    pl.semaphore_wait(barrier, n - 1)


def first_kernel(
    n, x_ref, g_ref, sw_ref, dw_ref, count_ref, x_out, gp_out, dx_out,
    xs, gs, gp, dx, weff, swb, dwb,
    up_sem, down_sem, side_sem, x_sem, gsend_sem, g_sem, load_sem, own_sem, out_sem,
):
    me = lax.axis_index("fsdp")
    nz = n // 2
    z, c = lax.div(me, 2), lax.rem(me, 2)
    rows, depth = x_ref.shape
    width = sw_ref.shape[1]
    tile = swb.shape[1]

    entry_barrier("fsdp", me, n)

    def slot(buf, chip, core):
        return buf.at[chip, pl.ds(pl.multiple_of(core * rows, rows), rows)]

    def x_copy(src, chip, core, sem, target):
        return pltpu.make_async_remote_copy(
            src_ref=src,
            dst_ref=slot(xs, chip, core),
            send_sem=sem.at[chip],
            recv_sem=x_sem.at[chip * 2 + core],
            device_id={"fsdp": target},
            device_id_type=MESH,
        )

    def g_copy(target):
        cols = pl.ds(pl.multiple_of(target * width, width), width)
        return pltpu.make_async_remote_copy(
            src_ref=g_ref.at[:, cols],
            dst_ref=slot(gs, z, c),
            send_sem=gsend_sem.at[target],
            recv_sem=g_sem.at[me],
            device_id={"fsdp": target},
            device_id_type=MESH,
        )

    up, down, sibling = me + 2, me - 2, z * 2 + (1 - c)

    @pl.when(z + 1 < nz)
    def _():
        x_copy(x_ref, z, c, up_sem, up).start()

    @pl.when(z > 0)
    def _():
        x_copy(x_ref, z, c, down_sem, down).start()

    x_copy(x_ref, z, c, side_sem, sibling).start()

    g_copy(sibling).start()

    def send_g(distance, carry):
        @pl.when(z - distance >= 0)
        def _():
            for core in range(2):
                g_copy((z - distance) * 2 + core).start()

        @pl.when(z + distance < nz)
        def _():
            for core in range(2):
                g_copy((z + distance) * 2 + core).start()

        return carry

    own_x = pltpu.make_async_copy(x_ref, slot(xs, z, c), own_sem.at[0])
    own_g = pltpu.make_async_copy(
        g_ref.at[:, pl.ds(pl.multiple_of(me * width, width), width)], slot(gs, z, c), own_sem.at[1]
    )
    own_x.start()
    own_g.start()

    def load(i, b):
        at = pl.ds(pl.multiple_of(i * tile, tile), tile)
        return (
            pltpu.make_async_copy(sw_ref.at[at], swb.at[b], load_sem.at[b, 0]),
            pltpu.make_async_copy(dw_ref.at[at], dwb.at[b], load_sem.at[b, 1]),
        )

    tiles = depth // tile
    for copy in load(0, 0):
        copy.start()

    def make_weff(i, carry):
        b = lax.rem(i, 2)

        @pl.when(i + 1 < tiles)
        def _():
            for copy in load(i + 1, 1 - b):
                copy.start()

        for copy in load(i, b):
            copy.wait()
        at = pl.ds(pl.multiple_of(i * tile, tile), tile)
        weff[at, :] = (swb[b].astype(F32) * dwb[b].astype(F32)).astype(BF16)
        return carry

    lax.fori_loop(0, tiles, make_weff, 0)
    own_x.wait()
    own_g.wait()

    count = count_ref[0]
    wt = min(256, width)
    dt = min(512, depth)

    def out_copies(chip):
        return (
            pltpu.make_async_copy(xs.at[chip], x_out.at[chip], out_sem.at[chip, 0]),
            pltpu.make_async_copy(gp.at[chip], gp_out.at[chip], out_sem.at[chip, 1]),
            pltpu.make_async_copy(dx.at[chip], dx_out.at[chip], out_sem.at[chip, 2]),
        )

    def receive(chip, distance, forward, target, sem):
        @pl.when(distance > 0)
        def _():
            x_copy(slot(xs, chip, c), chip, c, side_sem, sibling).wait_recv()

            @pl.when(forward)
            def _():
                x_copy(slot(xs, chip, c), chip, c, sem, target).start()

            x_copy(slot(xs, chip, c), chip, c, side_sem, sibling).start()

    def compute(chip, distance):
        pltpu.make_async_remote_copy(
            src_ref=slot(xs, chip, 1 - c),
            dst_ref=slot(xs, chip, 1 - c),
            send_sem=side_sem.at[chip],
            recv_sem=x_sem.at[chip * 2 + 1 - c],
            device_id={"fsdp": sibling},
            device_id_type=MESH,
        ).wait_recv()
        copies = out_copies(chip)
        copies[0].start()

        def wait_g(core):
            pltpu.make_async_remote_copy(
                src_ref=slot(gs, chip, core),
                dst_ref=slot(gs, chip, core),
                send_sem=gsend_sem.at[me],
                recv_sem=g_sem.at[chip * 2 + core],
                device_id={"fsdp": sibling},
                device_id_type=MESH,
            ).wait_recv()

        wait_g(1 - c)

        @pl.when(distance > 0)
        def _():
            wait_g(c)

        def pre(i, carry):
            at = pl.ds(pl.multiple_of(i * wt, wt), wt)
            preact = jnp.dot(xs[chip], weff[:, at], preferred_element_type=F32)
            sigma = jax.nn.sigmoid(preact)
            position = chip * (2 * rows) + lax.broadcasted_iota(jnp.int32, preact.shape, 0)
            slope = gs[chip, :, at].astype(F32) * sigma * (1.0 + preact * (1.0 - sigma))
            gp[chip, :, at] = jnp.where(position < count, slope, 0.0).astype(BF16)
            return carry

        lax.fori_loop(0, width // wt, pre, 0)
        copies[1].start()

        def back(i, carry):
            at = pl.ds(pl.multiple_of(i * dt, dt), dt)
            dx[chip, :, at] = lax.dot_general(
                gp[chip], weff[at, :], (((1,), (1,)), ((), ())), preferred_element_type=F32
            ).astype(BF16)
            return carry

        lax.fori_loop(0, depth // dt, back, 0)
        copies[2].start()

    lag = jnp.where((z > 0) & (z < nz - 1), 1, 0)

    def step(distance, carry):
        below, above = z - distance, z + distance
        has_below = (below >= 0) & (distance > 0)
        has_above = above < nz

        @pl.when(has_below)
        def _():
            receive(below, distance, z + 1 < nz, up, up_sem)

        @pl.when(has_above)
        def _():
            receive(above, distance, z > 0, down, down_sem)

        @pl.when(distance == 1)
        def _():
            lax.fori_loop(1, nz, send_g, 0)

        late = distance - lag

        @pl.when((late > 0) & (z - late >= 0))
        def _():
            compute(z - late, late)

        @pl.when((late >= 0) & (z + late < nz))
        def _():
            compute(z + late, late)

        return carry

    lax.fori_loop(0, nz + 1, step, 0)

    def finish(chip, carry):
        @pl.when((chip <= z) & (z + 1 < nz))
        def _():
            x_copy(slot(xs, chip, c), chip, c, up_sem, up).wait_send()

        @pl.when((chip >= z) & (z > 0))
        def _():
            x_copy(slot(xs, chip, c), chip, c, down_sem, down).wait_send()

        x_copy(slot(xs, chip, c), chip, c, side_sem, sibling).wait_send()
        for copy in out_copies(chip):
            copy.wait()
        return carry

    lax.fori_loop(0, nz, finish, 0)

    def finish_g(k, carry):
        g_copy(lax.rem(me + k, n)).wait_send()
        return carry

    lax.fori_loop(1, n, finish_g, 0)


def forward_and_input_grad(n, x, g, sw, dw, count):
    rows, depth = x.shape
    width = sw.shape[1]
    nz = n // 2
    tile = min(256, depth)
    whole = jax.ShapeDtypeStruct((nz, 2 * rows, depth), BF16)
    cols = jax.ShapeDtypeStruct((nz, 2 * rows, width), BF16)
    any_spec = pl.BlockSpec(memory_space=pl.ANY)
    dma = pltpu.SemaphoreType.DMA
    return pl.pallas_call(
        functools.partial(first_kernel, n),
        out_shape=(whole, cols, whole),
        in_specs=[any_spec] * 4 + [pl.BlockSpec(memory_space=pltpu.SMEM)],
        out_specs=(any_spec,) * 3,
        scratch_shapes=[
            pltpu.VMEM(whole.shape, BF16),
            pltpu.VMEM(cols.shape, BF16),
            pltpu.VMEM(cols.shape, BF16),
            pltpu.VMEM(whole.shape, BF16),
            pltpu.VMEM((depth, width), BF16),
            pltpu.VMEM((2, tile, width), BF16),
            pltpu.VMEM((2, tile, width), BF16),
            dma((nz,)),
            dma((nz,)),
            dma((nz,)),
            dma((n,)),
            dma((n,)),
            dma((n,)),
            dma((2, 2)),
            dma((2,)),
            dma((nz, 3)),
        ],
        compiler_params=pltpu.CompilerParams(
            collective_id=0, has_side_effects=True, vmem_limit_bytes=60 * 1024 * 1024
        ),
        name="gather_and_backprop",
    )(x, g, sw, dw, count)


def second_kernel(
    n, nd, x_ref, gp_ref, dx_ref, sw_ref, dw_ref, count_ref, shared_out, dom_out, in_out,
    xv, gv, tb, rb, acc, sib, chain, swb,
    load_sem, acc_sem, sib_send, sib_recv, ch_send, ch_recv, d_send, d_recv, sw_sem, dw_sem, out_sem,
):
    me, dom = lax.axis_index("fsdp"), lax.axis_index("dom")
    nz = n // 2
    z, c = lax.div(me, 2), lax.rem(me, 2)
    sibling = z * 2 + (1 - c)
    bits = nd.bit_length() - 1
    parts = min(2, bits)
    rows = in_out.shape[0]
    width = gv.shape[1]
    half = width // parts
    block = shared_out.shape[0]
    tile = min(256, block)
    pieces = block // tile

    def flip(value, mask):
        for b in range(bits):
            if mask >> b & 1:
                value = value + (1 << b) - (2 << b) * lax.rem(lax.div(value, 1 << b), 2)
        return value

    order = sorted(range(nd), key=lambda m: (-bin(m).count("1"), m))

    def bit_order(p):
        return [(p + s) % bits for s in range(bits)]

    def sent_at(m, p):
        return next((s for s, b in enumerate(bit_order(p)) if m >> b & 1), bits)

    index = {}
    for p in range(parts):
        for m in range(1, nd):
            s = sent_at(m, p)
            index[p, s, m ^ (1 << bit_order(p)[s])] = len(index)

    def block_rows(m, q):
        return pl.ds(pl.multiple_of(flip(dom, m) * block + q * tile, tile), tile)

    def part(p):
        return pl.ds(p * half, half)

    def piece_rows(q):
        return pl.ds(pl.multiple_of(q * tile, tile), tile)

    def d_copy(m, p, q):
        s = sent_at(m, p)
        bit = 1 << bit_order(p)[s]
        at = index[p, s, m ^ bit]
        return pltpu.make_async_remote_copy(
            src_ref=tb.at[block_rows(m, q), part(p)],
            dst_ref=rb.at[at, piece_rows(q)],
            send_sem=d_send.at[at, q],
            recv_sem=d_recv.at[at, q],
            device_id={"dom": flip(dom, bit)},
            device_id_type=MESH,
        )

    def arrived(m, p, q, steps):
        total = tb[block_rows(m, q), part(p)].astype(F32)
        for s in range(steps):
            at = index[p, s, m]
            pltpu.make_async_remote_copy(
                src_ref=rb.at[at, piece_rows(q)],
                dst_ref=rb.at[at, piece_rows(q)],
                send_sem=d_send.at[at, q],
                recv_sem=d_recv.at[at, q],
                device_id={"dom": flip(dom, 1 << bit_order(p)[s])},
                device_id_type=MESH,
            ).wait_recv()
            total = total + rb[at, piece_rows(q), :].astype(F32)
        return total

    def whole_block(m):
        return pl.ds(pl.multiple_of(flip(dom, m) * block, block), block)

    def sw_load(i):
        return pltpu.make_async_copy(
            sw_ref.at[whole_block(order[i])], swb.at[i % 2], sw_sem.at[i]
        )

    def dw_load(i):
        at = whole_block(order[i])
        return pltpu.make_async_copy(dw_ref.at[at], tb.at[at], dw_sem.at[i])

    def dom_store(i):
        return pltpu.make_async_copy(
            swb.at[i % 2], dom_out.at[whole_block(order[i])], out_sem.at[i]
        )

    def x_load(i):
        at = whole_block(order[i])
        return pltpu.make_async_copy(x_ref.at[:, at], xv.at[:, at], load_sem.at[i])

    load_g = pltpu.make_async_copy(gp_ref, gv, load_sem.at[nd])
    load_g.start()
    x_load(0).start()
    sw_load(0).start()
    dw_load(0).start()

    barrier = pltpu.get_barrier_semaphore()
    for b in range(bits):
        pl.semaphore_signal(
            barrier, inc=1, device_id={"dom": flip(dom, 1 << b)}, device_id_type=MESH
        )
    for near in (lax.rem(me + 2, n), lax.rem(me + n - 2, n), sibling):
        pl.semaphore_signal(barrier, inc=1, device_id={"fsdp": near}, device_id_type=MESH)
    pl.semaphore_wait(barrier, bits + 3)

    def own_rows(chip):
        return dx_ref.at[chip, pl.ds(pl.multiple_of(c * rows, rows), rows)]

    def acc_load(chip):
        return pltpu.make_async_copy(own_rows(chip), acc.at[chip], acc_sem.at[chip])

    def sib_copy(chip):
        return pltpu.make_async_remote_copy(
            src_ref=dx_ref.at[chip, pl.ds(pl.multiple_of((1 - c) * rows, rows), rows)],
            dst_ref=sib.at[chip],
            send_sem=sib_send.at[chip],
            recv_sem=sib_recv.at[chip],
            device_id={"fsdp": sibling},
            device_id_type=MESH,
        )

    def chain_copy(slot, chip, target):
        return pltpu.make_async_remote_copy(
            src_ref=acc.at[chip],
            dst_ref=chain.at[slot],
            send_sem=ch_send.at[chip],
            recv_sem=ch_recv.at[slot],
            device_id={"fsdp": target},
            device_id_type=MESH,
        )

    def send_up(chip):
        return chain_copy(chip, chip, lax.rem(me + 2, n))

    def send_down(chip):
        slot = jnp.where(chip == z - 1, nz, chip)
        return chain_copy(slot, chip, lax.rem(me + n - 2, n))

    def pair_order(k):
        return jnp.where(z == 0, nz - 1 - k, k)

    def start_sib(k, carry):
        chip = pair_order(k)
        sib_copy(chip).start()
        acc_load(chip).start()
        return carry

    lax.fori_loop(0, nz, start_sib, 0)

    scale = lax.rsqrt(jnp.full((1, 1), count_ref[0], jnp.int32).astype(F32))

    def weight_block(i):
        m = order[i]
        if i + 1 < nd:
            if i >= 1:
                dom_store(i - 1).wait()
            sw_load(i + 1).start()
        sw_load(i).wait()
        dw_load(i).wait()
        x_load(i).wait()

        def one(q, carry):
            at = block_rows(m, q)
            scaled = scale * lax.dot_general(
                xv[:, at], gv[...], (((0,), (0,)), ((), ())), preferred_element_type=F32
            )
            tb[at, :] = (scaled * tb[at, :].astype(F32)).astype(BF16)
            for p in range(parts):
                if sent_at(m, p) == 0:
                    d_copy(m, p, q).start()
            here = piece_rows(q)
            swb[i % 2, here, :] = (scaled * swb[i % 2, here, :].astype(F32)).astype(BF16)
            return carry

        lax.fori_loop(0, pieces, one, 0)
        dom_store(i).start()

    def pair_sum(k, carry):
        def add(chip):
            acc_load(chip).wait()
            sib_copy(chip).wait_recv()
            acc[chip] = (acc[chip].astype(F32) + sib[chip].astype(F32)).astype(BF16)

        chip = pair_order(k)
        add(chip)

        @pl.when((z == 0) & (chip > z))
        def _():
            send_up(chip).start()

        @pl.when((z == nz - 1) & (chip < z))
        def _():
            send_down(chip).start()

        return carry

    for i in range(1, nd):
        x_load(i).start()
        dw_load(i).start()
    pair_sum(0, 0)
    load_g.wait()
    weight_block(0)
    lax.fori_loop(1, nz, pair_sum, 0)

    for i in range(1, nd):
        weight_block(i)

    def hop(t, carry):
        def take(slot, chip):
            pltpu.make_async_remote_copy(
                src_ref=chain.at[slot],
                dst_ref=chain.at[slot],
                send_sem=ch_send.at[chip],
                recv_sem=ch_recv.at[slot],
                device_id={"fsdp": sibling},
                device_id_type=MESH,
            ).wait_recv()
            acc[chip] = (acc[chip].astype(F32) + chain[slot].astype(F32)).astype(BF16)

        rising = nz - 1 - (t - z)
        falling = t - (nz - 1 - z)

        @pl.when((z > 0) & (t >= z))
        def _():
            take(rising, rising)

            @pl.when(rising > z)
            def _():
                send_up(rising).start()

        @pl.when((z < nz - 1) & (falling >= 0))
        def _():
            take(jnp.where(falling == z, nz, falling), falling)

            @pl.when(falling < z)
            def _():
                send_down(falling).start()

        return carry

    if nz > 2:
        hop(1, 0)
    for s in range(1, bits):
        for m in order:
            for p in range(parts):
                if m and sent_at(m, p) == s:

                    def relay(q, carry, m=m, p=p, s=s):
                        total = arrived(m, p, q, s).astype(BF16)
                        tb[block_rows(m, q), part(p)] = total
                        d_copy(m, p, q).start()
                        return carry

                    lax.fori_loop(0, pieces, relay, 0)

    lax.fori_loop(2, nz - 1, hop, 0)

    def final(q, carry):
        for p in range(parts):
            shared_out[piece_rows(q), part(p)] = arrived(0, p, q, bits)
        return carry

    lax.fori_loop(0, pieces, final, 0)
    if nz > 1:
        hop(nz - 1, 0)
    in_out[...] = acc[z]

    for i in range(max(0, nd - 2), nd):
        dom_store(i).wait()
    for m in range(1, nd):
        for p in range(parts):

            def drain(q, carry, m=m, p=p):
                d_copy(m, p, q).wait_send()
                return carry

            lax.fori_loop(0, pieces, drain, 0)

    def drain_chain(chip, carry):
        sib_copy(chip).wait_send()

        @pl.when(chip > z)
        def _():
            send_up(chip).wait_send()

        @pl.when(chip < z)
        def _():
            send_down(chip).wait_send()

        return carry

    lax.fori_loop(0, nz, drain_chain, 0)


def weight_grads(n, nd, x, gp, dx, sw, dw, count):
    depth, width = sw.shape
    total = x.shape[0]
    rows = total // n
    nz = n // 2
    bits = nd.bit_length() - 1
    parts = min(2, bits)
    block = depth // nd
    pieces = block // min(256, block)
    buffers = parts * (nd - 1)
    any_spec = pl.BlockSpec(memory_space=pl.ANY)
    vmem_spec = pl.BlockSpec(memory_space=pltpu.VMEM)
    dma = pltpu.SemaphoreType.DMA
    return pl.pallas_call(
        functools.partial(second_kernel, n, nd),
        out_shape=(
            jax.ShapeDtypeStruct((block, width), F32),
            jax.ShapeDtypeStruct((depth, width), BF16),
            jax.ShapeDtypeStruct((rows, depth), BF16),
        ),
        in_specs=[any_spec] * 5 + [pl.BlockSpec(memory_space=pltpu.SMEM)],
        out_specs=(vmem_spec, any_spec, vmem_spec),
        scratch_shapes=[
            pltpu.VMEM((total, depth), BF16),
            pltpu.VMEM((total, width), BF16),
            pltpu.VMEM((depth, width), BF16),
            pltpu.VMEM((buffers, block, width // parts), BF16),
            pltpu.VMEM((nz, rows, depth), BF16),
            pltpu.VMEM((nz, rows, depth), BF16),
            pltpu.VMEM((nz + 1, rows, depth), BF16),
            pltpu.VMEM((2, block, width), BF16),
            dma((nd + 1,)),
            dma((nz,)),
            dma((nz,)),
            dma((nz,)),
            dma((nz,)),
            dma((nz + 1,)),
            dma((buffers, pieces)),
            dma((buffers, pieces)),
            dma((nd,)),
            dma((nd,)),
            dma((nd,)),
        ],
        compiler_params=pltpu.CompilerParams(
            collective_id=1, has_side_effects=True, vmem_limit_bytes=62 * 1024 * 1024
        ),
        name="weight_grads",
    )(x, gp, dx, sw, dw, count)


def store_kernel(a_ref, b_ref, c_ref, a_out, b_out, c_out):
    a_out[...] = a_ref[...]
    b_out[...] = b_ref[...]
    c_out[...] = c_ref[...]


def store_results(*arrays):
    steps = 8
    specs = tuple(
        pl.BlockSpec((a.shape[0] // steps, a.shape[1]), lambda i: (i, 0)) for a in arrays
    )
    return pl.pallas_call(
        store_kernel,
        grid=(steps,),
        out_shape=tuple(jax.ShapeDtypeStruct(a.shape, a.dtype) for a in arrays),
        in_specs=specs,
        out_specs=specs,
        compiler_params=pltpu.CompilerParams(vmem_limit_bytes=63 * 1024 * 1024),
        name="store_results",
    )(*arrays)


def solution(mesh):
    n, nd = mesh.shape["fsdp"], mesh.shape["dom"]

    def body(inputs, cotangent, shared_weight, domain_weight, row_counts):
        piece, grad_pre, partial = forward_and_input_grad(
            n, inputs[0], cotangent[0], shared_weight, domain_weight[0], row_counts
        )
        depth = piece.shape[-1]
        piece = piece.reshape(-1, depth)
        grad_pre = grad_pre.reshape(piece.shape[0], -1)
        shared_grad, domain_grad, input_grad = weight_grads(
            n, nd, piece, grad_pre, partial, shared_weight, domain_weight[0], row_counts
        )
        shared_grad, domain_grad, input_grad = store_results(
            shared_grad, domain_grad, input_grad
        )
        return (shared_grad, domain_grad[None], input_grad[None])

    return jax.shard_map(
        body,
        mesh=mesh,
        in_specs=(
            P("dom", "fsdp", None),
            P("dom", "fsdp", None),
            P(None, "fsdp"),
            P("dom", None, "fsdp"),
            P("dom"),
        ),
        out_specs=(P("dom", "fsdp"), P("dom", None, "fsdp"), P("dom", "fsdp", None)),
        check_vma=False,
    )
```

profile of v0, /device:TPU:12, one launch (start us, length us, event | category | flops | bytes accessed | tf_op | source)
XLA Modules:
  0.0 212.1 jit_solution(10111400138759788196)
XLA Ops:
  1.3 107.3 %gather_and_backprop.1 = (bf16[4,256,4096]{2,1,0:T(8,128)(2,1)}, bf16[4,256,1024]{2,1,0:T(8,128)(2,1)}, bf16[4,256,4096]{2,1,0:T(8,128)(2,1)}) custom-call(bf16[128,4096]{1,0:T(8,128)(2,1)} %bitcast.12, bf16[128,8192]{1,0:T(8,128)(2,1)} %bitcast.11, bf16[4096,1024]{1,0:T(8,128)(2,1)} %sw_ref.3, bf16[4096,1024]{1,0:T(8,128)(2,1)} %bitcast.7, s32[1]{0:T(128)S(6)} %copy.8.count_ref), custom_call_target="tpu_custom_call" | custom-call | tf_op jit(solution)/shard_map/gather_and_backprop/pallas_call | solution.py:266
  108.6 91.8 %weight_grads.1 = (f32[1024,1024]{1,0:T(8,128)}, bf16[4096,1024]{1,0:T(8,128)(2,1)}, bf16[128,4096]{1,0:T(8,128)(2,1)}) custom-call(bf16[1024,4096]{1,0:T(8,128)(2,1)} %bitcast.9, bf16[1024,1024]{1,0:T(8,128)(2,1)} %bitcast.10, bf16[4,256,4096]{2,1,0:T(8,128)(2,1)} %get-tuple-element.14.dx_ref, bf16[4096,1024]{1,0:T(8,128)(2,1)} %sw_ref.3, ...), custom_call_target="tpu_custom_call" | custom-call | tf_op jit(solution)/shard_map/weight_grads/pallas_call | solution.py:609
  200.4 11.7 %store_results.1 = (f32[1024,1024]{1,0:T(8,128)}, bf16[4096,1024]{1,0:T(8,128)(2,1)}, bf16[128,4096]{1,0:T(8,128)(2,1)}) custom-call(f32[1024,1024]{1,0:T(8,128)} %get-tuple-element.15.a_ref, bf16[4096,1024]{1,0:T(8,128)(2,1)} %get-tuple-element.16.b_ref, bf16[128,4096]{1,0:T(8,128)(2,1)} %get-tuple-element.17.c_ref), custom_call_target="tpu_custom_call" | custom-call | tf_op jit(solution)/shard_map/store_results/pallas_call | solution.py:657
where the time goes:
time: 215 us; the launch traced here: 212 us
  Pallas kernels  211 us (98%)
    pallas_call x1, Pallas kernels, forward_and_input_grad(): pl.pallas_call(functools.partial(first_kernel, n), out_shape=(whole, cols...  107 us
    pallas_call x1, Pallas kernels, weight_grads(): pl.pallas_call(functools.partial(second_kernel, n, nd), out_shape=(jax.Sh...  91.8 us
    pallas_call x1, Pallas kernels, store_results(): pl.pallas_call(store_kernel, grid=(steps,), out_shape=tuple((jax.ShapeDty...  11.7 us

commit v1 on v0

v1 whole, which is shorter than its diff:
```python
import functools

import jax
import jax.numpy as jnp
from jax import lax
from jax.experimental import pallas as pl
from jax.experimental.pallas import tpu as pltpu
from jax.sharding import PartitionSpec as P

MESH = pl.DeviceIdType.MESH
F32 = jnp.float32
BF16 = jnp.bfloat16
CHUNKS = 4
PIECES = 8
PAIR = 2
HALVES = 2
TILE = 256


def fused_kernel(
    n, nd, x_ref, g_ref, sw_ref, dw_ref, count_ref, shared_out, dom_out, in_out,
    xs, gs, weff, tb, rb, sib, chain, dxb, swb, shv,
    up_sem, down_sem, side_sem, x_sem, gsend_sem, g_sem, own_sem, sw_sem, dw_sem,
    sib_send, sib_recv, ch_send, ch_recv, d_send, d_recv, dom_sem, out_sem, in_sem, ready,
):
    me, dom = lax.axis_index("fsdp"), lax.axis_index("dom")
    nz = n // 2
    z, c = lax.div(me, 2), lax.rem(me, 2)
    up, down, sibling = me + 2, me - 2, z * 2 + (1 - c)
    rows, depth = x_ref.shape
    width = sw_ref.shape[1]
    cw = width // CHUNKS
    pw = depth // PIECES
    block = depth // nd
    bits = nd.bit_length() - 1
    parts = min(2, bits)
    tile = min(TILE, block // parts)
    pieces = block // tile

    def flip(value, mask):
        for b in range(bits):
            if mask >> b & 1:
                value = value + (1 << b) - (2 << b) * lax.rem(lax.div(value, 1 << b), 2)
        return value

    barrier = pltpu.get_barrier_semaphore()

    def greet(k, carry):
        pl.semaphore_signal(
            barrier, inc=1, device_id={"fsdp": lax.rem(me + k, n)}, device_id_type=MESH
        )
        return carry

    lax.fori_loop(1, n, greet, 0)
    for b in range(bits):
        pl.semaphore_signal(
            barrier, inc=1, device_id={"dom": flip(dom, 1 << b)}, device_id_type=MESH
        )

    def cols(j):
        return pl.ds(pl.multiple_of(j * cw, cw), cw)

    def depth_cols(pc):
        return pl.ds(pl.multiple_of(pc * pw, pw), pw)

    def chip_rows(chip):
        return pl.ds(pl.multiple_of(chip * (2 * rows), 2 * rows), 2 * rows)

    def core_rows(chip, core):
        return pl.ds(pl.multiple_of((chip * 2 + core) * rows, rows), rows)

    def sw_load(j):
        return pltpu.make_async_copy(sw_ref.at[:, cols(j)], swb.at[lax.rem(j, 2)], sw_sem.at[j])

    def dw_load(j):
        return pltpu.make_async_copy(dw_ref.at[:, cols(j)], tb.at[j], dw_sem.at[j])

    own_x = pltpu.make_async_copy(x_ref, xs.at[core_rows(z, c)], own_sem.at[0])
    own_g = pltpu.make_async_copy(
        g_ref.at[:, pl.ds(pl.multiple_of(me * width, width), width)],
        gs.at[core_rows(z, c)],
        own_sem.at[1],
    )
    for j in range(CHUNKS):
        if j < 2:
            sw_load(j).start()
        dw_load(j).start()
    own_x.start()
    own_g.start()

    pl.semaphore_wait(barrier, n - 1 + bits)

    part = rows // HALVES

    def x_slot(chip, core, h):
        at = (chip * 2 + core) * rows + h * part
        return xs.at[pl.ds(pl.multiple_of(at, part), part)]

    def x_copy(src, chip, core, h, sem, target):
        return pltpu.make_async_remote_copy(
            src_ref=src,
            dst_ref=x_slot(chip, core, h),
            send_sem=sem.at[chip, h],
            recv_sem=x_sem.at[chip * 2 + core, h],
            device_id={"fsdp": target},
            device_id_type=MESH,
        )

    def g_copy(target, j):
        at = pl.ds(pl.multiple_of(target * width + j * cw, cw), cw)
        return pltpu.make_async_remote_copy(
            src_ref=g_ref.at[:, at],
            dst_ref=gs.at[core_rows(z, c), cols(j)],
            send_sem=gsend_sem.at[target, j],
            recv_sem=g_sem.at[me, j],
            device_id={"fsdp": target},
            device_id_type=MESH,
        )

    for h in range(HALVES):
        mine = x_ref.at[pl.ds(h * part, part)]

        @pl.when(z + 1 < nz)
        def _():
            x_copy(mine, z, c, h, up_sem, up).start()

        @pl.when(z > 0)
        def _():
            x_copy(mine, z, c, h, down_sem, down).start()

        x_copy(mine, z, c, h, side_sem, sibling).start()

    def each_chunk(body):
        def step(j, carry):
            body(j)
            return carry

        lax.fori_loop(0, CHUNKS, step, 0)

    each_chunk(lambda j: g_copy(sibling, j).start())

    def send_g_near(chip):
        def one(j):
            for core in range(2):
                g_copy(chip * 2 + core, j).start()

        each_chunk(one)

    def is_end(chip):
        return (chip == 0) | (chip == nz - 1)

    def is_far(chip):
        return (chip >= 0) & (chip < nz) & ((chip > z + 1) | (chip < z - 1))

    def send_g_middle(j):
        def one(chip, carry):
            @pl.when(is_far(chip))
            def _():
                for core in range(2):
                    g_copy(chip * 2 + core, j).start()

            return carry

        lax.fori_loop(1, nz - 1, one, 0)

    def send_g_end(level, first, last):
        for chip in (0, nz - 1):

            @pl.when(is_far(chip))
            def _():
                pl.semaphore_wait(ready.at[level, chip], 2)

                def one(j, carry):
                    for core in range(2):
                        g_copy(chip * 2 + core, j).start()
                    return carry

                lax.fori_loop(first, last, one, 0)

    def tell_far(level):
        def one(chip, carry):
            @pl.when(is_far(chip))
            def _():
                for core in range(2):
                    pl.semaphore_signal(
                        ready.at[level, z],
                        inc=1,
                        device_id={"fsdp": chip * 2 + core},
                        device_id_type=MESH,
                    )

            return carry

        @pl.when(is_end(z))
        def _():
            lax.fori_loop(0, nz, one, 0)

    et = min(512, depth)

    def make_weff(j):
        sw_load(j).wait()
        dw_load(j).wait()

        def one(i, carry):
            at = pl.ds(pl.multiple_of(i * et, et), et)
            weff[at, cols(j)] = (
                swb[lax.rem(j, 2), at, :].astype(F32) * tb[j, at, :].astype(F32)
            ).astype(BF16)
            return carry

        lax.fori_loop(0, depth // et, one, 0)

        @pl.when(j + 2 < CHUNKS)
        def _():
            sw_load(j + 2).start()

    each_chunk(make_weff)
    for j in range(2):
        sw_load(j).start()
    own_x.wait()
    own_g.wait()

    count = count_ref[0]
    scale = lax.rsqrt(jnp.full((1, 1), count, jnp.int32).astype(F32))

    def wait_x_half(chip, core, h):
        slot = x_slot(chip, core, h)
        x_copy(slot, chip, core, h, side_sem, sibling).wait_recv()

    def wait_x(chip, core):
        for h in range(HALVES):
            wait_x_half(chip, core, h)

    def wait_g(chip, core, j):
        pltpu.make_async_remote_copy(
            src_ref=gs.at[core_rows(chip, core), cols(j)],
            dst_ref=gs.at[core_rows(chip, core), cols(j)],
            send_sem=gsend_sem.at[me, j],
            recv_sem=g_sem.at[chip * 2 + core, j],
            device_id={"fsdp": sibling},
            device_id_type=MESH,
        ).wait_recv()

    def pre(chip, j):
        wait_g(chip, 1 - c, j)

        @pl.when(chip != z)
        def _():
            wait_g(chip, c, j)

        here = chip_rows(chip)
        preact = jnp.dot(xs[here, :], weff[:, cols(j)], preferred_element_type=F32)
        sigma = jax.nn.sigmoid(preact)
        position = chip * (2 * rows) + lax.broadcasted_iota(jnp.int32, preact.shape, 0)
        slope = gs[here, cols(j)].astype(F32) * sigma * (1.0 + preact * (1.0 - sigma))
        gs[here, cols(j)] = jnp.where(position < count, slope, 0.0).astype(BF16)

    def sib_copy(chip, slot, pc):
        return pltpu.make_async_remote_copy(
            src_ref=dxb.at[slot, pc, pl.ds(pl.multiple_of((1 - c) * rows, rows), rows)],
            dst_ref=sib.at[chip, pc],
            send_sem=sib_send.at[chip, pc],
            recv_sem=sib_recv.at[chip, pc],
            device_id={"fsdp": sibling},
            device_id_type=MESH,
        )

    def chain_copy(slot, chip, pc, target):
        return pltpu.make_async_remote_copy(
            src_ref=sib.at[chip, pc],
            dst_ref=chain.at[slot, pc],
            send_sem=ch_send.at[chip, pc],
            recv_sem=ch_recv.at[slot, pc],
            device_id={"fsdp": target},
            device_id_type=MESH,
        )

    def send_up(chip, pc):
        return chain_copy(chip, chip, pc, lax.rem(me + 2, n))

    def send_down(chip, pc):
        return chain_copy(jnp.where(chip == z - 1, nz, chip), chip, pc, lax.rem(me + n - 2, n))

    def pair_sum(chip, slot, pc):
        sib_copy(chip, slot, pc).wait_send()
        sib_copy(chip, slot, pc).wait_recv()
        own = dxb[slot, pc, pl.ds(pl.multiple_of(c * rows, rows), rows), :]
        sib[chip, pc] = (own.astype(F32) + sib[chip, pc].astype(F32)).astype(BF16)

        @pl.when((z == 0) & (chip > z))
        def _():
            send_up(chip, pc).start()

        @pl.when((z == nz - 1) & (chip < z))
        def _():
            send_down(chip, pc).start()

    def each_piece(body):
        def step(pc, carry):
            body(pc)
            return carry

        lax.fori_loop(0, PIECES, step, 0)

    def back(chip, turn, before, pending):
        slot = lax.rem(turn, 2)

        def one(group, carry):
            wide = PAIR * pw
            at = pl.ds(pl.multiple_of(group * wide, wide), wide)
            partial = lax.dot_general(
                gs[chip_rows(chip), :],
                weff[at, :],
                (((1,), (1,)), ((), ())),
                preferred_element_type=F32,
            ).astype(BF16)
            for i in range(PAIR):
                pc = group * PAIR + i
                dxb[slot, pc] = partial[:, i * pw : (i + 1) * pw]
                sib_copy(chip, slot, pc).start()

            @pl.when(pending)
            def _():
                for i in range(PAIR):
                    pair_sum(before, 1 - slot, group * PAIR + i)

            return carry

        lax.fori_loop(0, PIECES // PAIR, one, 0)

    wait_x(z, 1 - c)
    each_chunk(lambda j: pre(z, j))
    back(z, 0, z, False)

    def receive(chip, h, forward, target, sem):
        wait_x_half(chip, c, h)
        slot = x_slot(chip, c, h)

        @pl.when(forward)
        def _():
            x_copy(slot, chip, c, h, sem, target).start()

        x_copy(slot, chip, c, h, side_sem, sibling).start()

    def receive_both(distance, h):
        below, above = z - distance, z + distance

        @pl.when(below >= 0)
        def _():
            receive(below, h, z + 1 < nz, up, up_sem)

        @pl.when(above < nz)
        def _():
            receive(above, h, z > 0, down, down_sem)

    @pl.when(z == 0)
    def _():
        send_g_near(z + 1)

    @pl.when(z == nz - 1)
    def _():
        send_g_near(z - 1)

    def gather_step(distance, carry):
        for h in range(HALVES):
            receive_both(distance, h)

        @pl.when((distance == 1) & (z > 0) & (z < nz - 1))
        def _():
            send_g_near(z + 1)
            send_g_near(z - 1)

        @pl.when(distance == nz - 2)
        def _():
            each_chunk(send_g_middle)

        return carry

    lax.fori_loop(1, nz - 1, gather_step, 0)

    def near(side, carry):
        turn, before = carry
        chip = z - 1 + 2 * side
        valid = (chip >= 0) & (chip < nz)

        @pl.when(valid)
        def _():
            wait_x(chip, 1 - c)
            each_chunk(lambda j: pre(chip, j))
            back(chip, turn, before, True)

        return jnp.where(valid, turn + 1, turn), jnp.where(valid, chip, before)

    turns, last = lax.fori_loop(0, 2, near, (1, z))

    for h in range(HALVES):
        receive_both(nz - 1, h)
        if h == 0:
            tell_far(0)
            send_g_end(0, 0, 1)
    tell_far(1)

    @pl.when(is_end(z))
    def _():
        send_g_end(1, 1, CHUNKS)

    def far_chip(k):
        chip = jnp.where(z < nz // 2, nz - 1 - k, k)
        return chip, is_far(chip)

    order = sorted(range(nd), key=lambda m: (-bin(m).count("1"), m))

    def bit_order(p):
        return [(p + s) % bits for s in range(bits)]

    def sent_at(m, p):
        return next((s for s, b in enumerate(bit_order(p)) if m >> b & 1), bits)

    index = [{} for _ in range(parts)]
    for p in range(parts):
        for m in range(1, nd):
            s = sent_at(m, p)
            index[p][s, m ^ (1 << bit_order(p)[s])] = len(index[p])

    def tile_rows(m, q):
        return pl.ds(pl.multiple_of(flip(dom, m) * block + q * tile, tile), tile)

    def block_rows(m):
        return pl.ds(pl.multiple_of(flip(dom, m) * block, block), block)

    def d_copy(j, m, q):
        p = q % parts
        s = sent_at(m, p)
        bit = 1 << bit_order(p)[s]
        at = index[p][s, m ^ bit]
        return pltpu.make_async_remote_copy(
            src_ref=tb.at[j, tile_rows(m, q)],
            dst_ref=rb.at[at, j, pl.ds(q * tile, tile)],
            send_sem=d_send.at[at, j, q],
            recv_sem=d_recv.at[at, j, q],
            device_id={"dom": flip(dom, bit)},
            device_id_type=MESH,
        )

    def arrived(j, m, q, steps):
        p = q % parts
        total = tb[j, tile_rows(m, q), :].astype(F32)
        for s in range(steps):
            at = index[p][s, m]
            here = pl.ds(q * tile, tile)
            pltpu.make_async_remote_copy(
                src_ref=rb.at[at, j, here],
                dst_ref=rb.at[at, j, here],
                send_sem=d_send.at[at, j, q],
                recv_sem=d_recv.at[at, j, q],
                device_id={"dom": flip(dom, 1 << bit_order(p)[s])},
                device_id_type=MESH,
            ).wait_recv()
            total = total + rb[at, j, here, :].astype(F32)
        return total

    def dom_store(j, m):
        return pltpu.make_async_copy(
            swb.at[lax.rem(j, 2), block_rows(m)],
            dom_out.at[block_rows(m), cols(j)],
            dom_sem.at[j, m],
        )

    def weight_chunk(j):
        sw_load(j).wait()

        @pl.when((j >= 1) & (j + 1 < CHUNKS))
        def _():
            for m in range(nd):
                dom_store(j - 1, m).wait()
            sw_load(j + 1).start()

        slot = lax.rem(j, 2)
        for m in order:
            at = block_rows(m)
            scaled = scale * lax.dot_general(
                xs[:, at], gs[:, cols(j)], (((0,), (0,)), ((), ())), preferred_element_type=F32
            )
            tb[j, at, :] = (scaled * tb[j, at, :].astype(F32)).astype(BF16)
            for q in range(pieces):
                if sent_at(m, q % parts) == 0:
                    d_copy(j, m, q).start()
            swb[slot, at, :] = (scaled * swb[slot, at, :].astype(F32)).astype(BF16)
            dom_store(j, m).start()

    def wait_far_x(k, carry):
        chip, valid = far_chip(k)

        @pl.when(valid)
        def _():
            wait_x(chip, 1 - c)

        return carry

    lax.fori_loop(0, nz, wait_far_x, 0)

    def chunk_step(j):
        @pl.when((j == CHUNKS // 2) & (z > 0) & (z < nz - 1))
        def _():
            send_g_end(1, 1, CHUNKS)

        def far_pre(k, carry):
            chip, valid = far_chip(k)

            @pl.when(valid)
            def _():
                pre(chip, j)

            return carry

        lax.fori_loop(0, nz, far_pre, 0)

        @pl.when(j == 0)
        def _():
            each_piece(lambda pc: pair_sum(last, lax.rem(turns - 1, 2), pc))

        @pl.when(j == CHUNKS - 1)
        def _():
            def far_back(k, carry):
                turn, before, pending = carry
                chip, valid = far_chip(k)

                @pl.when(valid)
                def _():
                    back(chip, turn, before, pending > 0)

                return (
                    jnp.where(valid, turn + 1, turn),
                    jnp.where(valid, chip, before),
                    jnp.where(valid, 1, pending),
                )

            turn, before, pending = lax.fori_loop(0, nz, far_back, (turns, last, 0))

            @pl.when(pending > 0)
            def _():
                each_piece(lambda pc: pair_sum(before, lax.rem(turn - 1, 2), pc))

        weight_chunk(j)

    each_chunk(chunk_step)

    hops = (nz - 1) * PIECES

    def take(slot, chip, pc):
        pltpu.make_async_remote_copy(
            src_ref=chain.at[slot, pc],
            dst_ref=chain.at[slot, pc],
            send_sem=ch_send.at[chip, pc],
            recv_sem=ch_recv.at[slot, pc],
            device_id={"fsdp": sibling},
            device_id_type=MESH,
        ).wait_recv()
        sib[chip, pc] = (sib[chip, pc].astype(F32) + chain[slot, pc].astype(F32)).astype(BF16)

    def turn_of(step):
        rising = jnp.where(step < PIECES, 1, nz - lax.div(step, PIECES))
        return rising, lax.rem(step, PIECES), (step >= 0) & (step < hops)

    def hop(t):
        rising, pc, valid = turn_of(t - (z - 1))

        @pl.when(valid & (z > 0) & (rising >= z))
        def _():
            take(rising, rising, pc)

            @pl.when(rising > z)
            def _():
                send_up(rising, pc).start()

        mirrored, pd, due = turn_of(t - (nz - 2 - z))
        falling = nz - 1 - mirrored

        @pl.when(due & (z < nz - 1) & (falling <= z))
        def _():
            take(jnp.where(falling == z, nz, falling), falling, pd)

            @pl.when(falling < z)
            def _():
                send_down(falling, pd).start()

    def relay(j):
        for s in range(1, bits):
            for m in order:
                for q in range(pieces):
                    if m and sent_at(m, q % parts) == s:
                        total = arrived(j, m, q, s).astype(BF16)
                        tb[j, tile_rows(m, q), :] = total
                        d_copy(j, m, q).start()

    def shared_store(j):
        return pltpu.make_async_copy(shv.at[j], shared_out.at[:, cols(j)], out_sem.at[j])

    spread = PIECES // 2

    def tail_step(t, carry):
        hop(t)
        mark = t - (PIECES - 1)

        @pl.when((mark >= 0) & (lax.rem(mark, spread) == 0) & (mark < spread * CHUNKS))
        def _():
            relay(lax.div(mark, spread))

        return carry

    lax.fori_loop(0, max(hops + nz - 2, PIECES - 1 + spread * CHUNKS), tail_step, 0)

    def in_store(pc):
        return pltpu.make_async_copy(sib.at[z, pc], in_out.at[:, depth_cols(pc)], in_sem.at[pc])

    each_piece(lambda pc: in_store(pc).start())

    def final(j):
        for q in range(pieces):
            shv[j, pl.ds(q * tile, tile), :] = arrived(j, 0, q, bits)
        shared_store(j).start()

    each_chunk(final)

    for j in range(max(0, CHUNKS - 2), CHUNKS):
        for m in range(nd):
            dom_store(j, m).wait()

    def drain_chip(chip, carry):
        for h in range(HALVES):
            slot = x_slot(chip, c, h)

            @pl.when((chip <= z) & (z + 1 < nz))
            def _():
                x_copy(slot, chip, c, h, up_sem, up).wait_send()

            @pl.when((chip >= z) & (z > 0))
            def _():
                x_copy(slot, chip, c, h, down_sem, down).wait_send()

            x_copy(slot, chip, c, h, side_sem, sibling).wait_send()

        def sums(pc):
            @pl.when(chip > z)
            def _():
                send_up(chip, pc).wait_send()

            @pl.when(chip < z)
            def _():
                send_down(chip, pc).wait_send()

        each_piece(sums)
        return carry

    lax.fori_loop(0, nz, drain_chip, 0)

    def drain_g(k, carry):
        each_chunk(lambda j: g_copy(lax.rem(me + k, n), j).wait_send())
        return carry

    lax.fori_loop(1, n, drain_g, 0)

    def drain_d(j):
        for m in range(1, nd):
            for q in range(pieces):
                d_copy(j, m, q).wait_send()
        shared_store(j).wait()

    each_chunk(drain_d)
    each_piece(lambda pc: in_store(pc).wait())


def fused(n, nd, x, g, sw, dw, count):
    rows, depth = x.shape
    width = sw.shape[1]
    nz = n // 2
    total = n * rows
    block = depth // nd
    bits = nd.bit_length() - 1
    tile = min(TILE, block // min(2, bits))
    pieces = block // tile
    cw, pw = width // CHUNKS, depth // PIECES
    any_spec = pl.BlockSpec(memory_space=pl.ANY)
    dma = pltpu.SemaphoreType.DMA
    vmem = pltpu.VMEM
    return pl.pallas_call(
        functools.partial(fused_kernel, n, nd),
        out_shape=(
            jax.ShapeDtypeStruct((block, width), F32),
            jax.ShapeDtypeStruct((depth, width), BF16),
            jax.ShapeDtypeStruct((rows, depth), BF16),
        ),
        in_specs=[any_spec] * 4 + [pl.BlockSpec(memory_space=pltpu.SMEM)],
        out_specs=(any_spec,) * 3,
        scratch_shapes=[
            vmem((total, depth), BF16),
            vmem((total, width), BF16),
            vmem((depth, width), BF16),
            vmem((CHUNKS, depth, cw), BF16),
            vmem((nd - 1, CHUNKS, block, cw), BF16),
            vmem((nz, PIECES, rows, pw), BF16),
            vmem((nz + 1, PIECES, rows, pw), BF16),
            vmem((2, PIECES, 2 * rows, pw), BF16),
            vmem((2, depth, cw), BF16),
            vmem((CHUNKS, block, cw), F32),
            dma((nz, HALVES)),
            dma((nz, HALVES)),
            dma((nz, HALVES)),
            dma((n, HALVES)),
            dma((n, CHUNKS)),
            dma((n, CHUNKS)),
            dma((2,)),
            dma((CHUNKS,)),
            dma((CHUNKS,)),
            dma((nz, PIECES)),
            dma((nz, PIECES)),
            dma((nz, PIECES)),
            dma((nz + 1, PIECES)),
            dma((nd - 1, CHUNKS, pieces)),
            dma((nd - 1, CHUNKS, pieces)),
            dma((CHUNKS, nd)),
            dma((CHUNKS,)),
            dma((PIECES,)),
            pltpu.SemaphoreType.REGULAR((2, nz)),
        ],
        compiler_params=pltpu.CompilerParams(
            collective_id=0, has_side_effects=True, vmem_limit_bytes=63 * 1024 * 1024
        ),
        name="gather_backprop_reduce",
    )(x, g, sw, dw, count)


def store_kernel(a_ref, b_ref, c_ref, a_out, b_out, c_out):
    a_out[...] = a_ref[...]
    b_out[...] = b_ref[...]
    c_out[...] = c_ref[...]


def store_results(*arrays):
    steps = 8
    specs = tuple(
        pl.BlockSpec((a.shape[0] // steps, a.shape[1]), lambda i: (i, 0)) for a in arrays
    )
    return pl.pallas_call(
        store_kernel,
        grid=(steps,),
        out_shape=tuple(jax.ShapeDtypeStruct(a.shape, a.dtype) for a in arrays),
        in_specs=specs,
        out_specs=specs,
        compiler_params=pltpu.CompilerParams(vmem_limit_bytes=63 * 1024 * 1024),
        name="store_results",
    )(*arrays)


def solution(mesh):
    n, nd = mesh.shape["fsdp"], mesh.shape["dom"]

    def body(inputs, cotangent, shared_weight, domain_weight, row_counts):
        results = fused(
            n, nd, inputs[0], cotangent[0], shared_weight, domain_weight[0], row_counts
        )
        shared_grad, domain_grad, input_grad = store_results(*results)
        return (shared_grad, domain_grad[None], input_grad[None])

    return jax.shard_map(
        body,
        mesh=mesh,
        in_specs=(
            P("dom", "fsdp", None),
            P("dom", "fsdp", None),
            P(None, "fsdp"),
            P("dom", None, "fsdp"),
            P("dom"),
        ),
        out_specs=(P("dom", "fsdp"), P("dom", None, "fsdp"), P("dom", "fsdp", None)),
        check_vma=False,
    )
```

time: 215 us -> 201 us (0.935); the launches traced: 212 us -> 201 us
  Pallas kernels: 211 us -> 200 us
    pallas_call x2 -> x1, Pallas kernels: 199 us -> 188 us  [fused(): pl.pallas_call(functools.partial(fused_kernel, n, nd), out_shape=(jax.Sha...]
where the time goes in v1:
time: 201 us
  Pallas kernels  200 us (100%)
    pallas_call x1, Pallas kernels, fused(): pl.pallas_call(functools.partial(fused_kernel, n, nd), out_shape=(jax.Sha...  188 us
    pallas_call x1, Pallas kernels, store_results(): pl.pallas_call(store_kernel, grid=(steps,), out_shape=tuple((jax.ShapeDty...  11.7 us

profile of v1, /device:TPU:12, one launch (start us, length us, event | category | flops | bytes accessed | tf_op | source)
XLA Modules:
  0.0 200.9 jit_solution(13167912056200725194)
XLA Ops:
  1.3 187.8 %gather_backprop_reduce.1 = (f32[1024,1024]{1,0:T(8,128)}, bf16[4096,1024]{1,0:T(8,128)(2,1)}, bf16[128,4096]{1,0:T(8,128)(2,1)}) custom-call(bf16[128,4096]{1,0:T(8,128)(2,1)} %bitcast.7, bf16[128,8192]{1,0:T(8,128)(2,1)} %bitcast.6, bf16[4096,1024]{1,0:T(8,128)(2,1)} %sw_ref.1, bf16[4096,1024]{1,0:T(8,128)(2,1)} %bitcast.5, s32[1]{0:T(128)S(6)} %copy.8.count_ref), custom_call_target="tpu_custom_call" | custom-call | tf_op jit(solution)/shard_map/gather_backprop_reduce/pallas_call | solution.py:686
  189.1 11.7 %store_results.1 = (f32[1024,1024]{1,0:T(8,128)}, bf16[4096,1024]{1,0:T(8,128)(2,1)}, bf16[128,4096]{1,0:T(8,128)(2,1)}) custom-call(f32[1024,1024]{1,0:T(8,128)} %get-tuple-element.9.a_ref, bf16[4096,1024]{1,0:T(8,128)(2,1)} %get-tuple-element.10.b_ref, bf16[128,4096]{1,0:T(8,128)(2,1)} %get-tuple-element.11.c_ref), custom_call_target="tpu_custom_call" | custom-call | tf_op jit(solution)/shard_map/store_results/pallas_call | solution.py:744

commit v2 on v1

--- a/solution.py
+++ b/solution.py
@@ -14,6 +14,8 @@
 PIECES = 8
 PAIR = 2
 HALVES = 2
+EARLY = 2
+STORES = 8
 TILE = 256
 
 
@@ -163,10 +165,12 @@
 
         lax.fori_loop(1, nz - 1, one, 0)
 
-    def send_g_end(level, first, last):
+    def send_g_end(level):
         for chip in (0, nz - 1):
-
-            @pl.when(is_far(chip))
+            across = is_end(z)
+            mine = jnp.logical_not(across) if level == 2 else True
+
+            @pl.when(is_far(chip) & mine)
             def _():
                 pl.semaphore_wait(ready.at[level, chip], 2)
 
@@ -175,11 +179,14 @@
                         g_copy(chip * 2 + core, j).start()
                     return carry
 
-                lax.fori_loop(first, last, one, 0)
+                until = (1, jnp.where(across, CHUNKS, 2), CHUNKS)[level]
+                lax.fori_loop(level, until, one, 0)
 
     def tell_far(level):
         def one(chip, carry):
-            @pl.when(is_far(chip))
+            theirs = jnp.logical_not(is_end(chip)) if level == 2 else True
+
+            @pl.when(is_far(chip) & theirs)
             def _():
                 for core in range(2):
                     pl.semaphore_signal(
@@ -393,20 +400,34 @@
 
     turns, last = lax.fori_loop(0, 2, near, (1, z))
 
+    def flush(chip, turn, first, last):
+        def one(pc, carry):
+            pair_sum(chip, lax.rem(turn, 2), pc)
+            return carry
+
+        lax.fori_loop(first, last, one, 0)
+
+    flush(last, turns - 1, 0, PIECES // 4)
     for h in range(HALVES):
         receive_both(nz - 1, h)
         if h == 0:
             tell_far(0)
-            send_g_end(0, 0, 1)
+            send_g_end(0)
+            flush(last, turns - 1, PIECES // 4, PIECES)
     tell_far(1)
 
     @pl.when(is_end(z))
     def _():
-        send_g_end(1, 1, CHUNKS)
-
-    def far_chip(k):
-        chip = jnp.where(z < nz // 2, nz - 1 - k, k)
-        return chip, is_far(chip)
+        send_g_end(1)
+
+    farthest = jnp.where(z < nz // 2, nz - 1, 0)
+
+    def each_far(body):
+        def one(k, carry):
+            chip = jnp.where(z < nz // 2, nz - 1 - k, k)
+            return body(chip, is_far(chip), carry)
+
+        return lambda carry: lax.fori_loop(0, nz, one, carry)
 
     order = sorted(range(nd), key=lambda m: (-bin(m).count("1"), m))
 
@@ -488,58 +509,74 @@
             swb[slot, at, :] = (scaled * swb[slot, at, :].astype(F32)).astype(BF16)
             dom_store(j, m).start()
 
-    def wait_far_x(k, carry):
-        chip, valid = far_chip(k)
-
+    def wait_far_x(chip, valid, carry):
         @pl.when(valid)
         def _():
             wait_x(chip, 1 - c)
 
         return carry
 
-    lax.fori_loop(0, nz, wait_far_x, 0)
+    each_far(wait_far_x)(0)
 
     def chunk_step(j):
-        @pl.when((j == CHUNKS // 2) & (z > 0) & (z < nz - 1))
-        def _():
-            send_g_end(1, 1, CHUNKS)
-
-        def far_pre(k, carry):
-            chip, valid = far_chip(k)
-
-            @pl.when(valid)
+        @pl.when((j == 1) & (z > 0) & (z < nz - 1))
+        def _():
+            send_g_end(1)
+
+        @pl.when((j == 2) & (z > 0) & (z < nz - 1))
+        def _():
+            send_g_end(2)
+
+        @pl.when(j <= EARLY)
+        def _():
+            def some(i, carry):
+                pre(farthest, i)
+                return carry
+
+            lax.fori_loop(j, jnp.where(j == EARLY, CHUNKS, j + 1), some, 0)
+
+        @pl.when(j == 0)
+        def _():
+            tell_far(2)
+
+        @pl.when(j == EARLY)
+        def _():
+            back(farthest, turns, farthest, False)
+
+        def far_pre(chip, valid, carry):
+            @pl.when(valid & (chip != farthest))
             def _():
                 pre(chip, j)
 
             return carry
 
-        lax.fori_loop(0, nz, far_pre, 0)
-
-        @pl.when(j == 0)
-        def _():
-            each_piece(lambda pc: pair_sum(last, lax.rem(turns - 1, 2), pc))
+        each_far(far_pre)(0)
+
+        @pl.when(j == EARLY)
+        def _():
+            flush(farthest, turns, 0, PIECES)
 
         @pl.when(j == CHUNKS - 1)
         def _():
-            def far_back(k, carry):
+            def far_back(chip, valid, carry):
                 turn, before, pending = carry
-                chip, valid = far_chip(k)
-
-                @pl.when(valid)
+                new = valid & (chip != farthest)
+
+                @pl.when(new)
                 def _():
                     back(chip, turn, before, pending > 0)
 
                 return (
-                    jnp.where(valid, turn + 1, turn),
-                    jnp.where(valid, chip, before),
-                    jnp.where(valid, 1, pending),
+                    jnp.where(new, turn + 1, turn),
+                    jnp.where(new, chip, before),
+                    jnp.where(new, 1, pending),
                 )
 
-            turn, before, pending = lax.fori_loop(0, nz, far_back, (turns, last, 0))
+            turn, before, pending = each_far(far_back)((turns + 1, farthest, 0))
 
             @pl.when(pending > 0)
             def _():
-                each_piece(lambda pc: pair_sum(before, lax.rem(turn - 1, 2), pc))
+                flush(before, turn - 1, 0, PIECES)
 
         weight_chunk(j)
 
@@ -559,7 +596,8 @@
         sib[chip, pc] = (sib[chip, pc].astype(F32) + chain[slot, pc].astype(F32)).astype(BF16)
 
     def turn_of(step):
-        rising = jnp.where(step < PIECES, 1, nz - lax.div(step, PIECES))
+        turn = lax.div(step, PIECES)
+        rising = jnp.where(turn == 0, 1, nz - turn)
         return rising, lax.rem(step, PIECES), (step >= 0) & (step < hops)
 
     def hop(t):
@@ -721,7 +759,7 @@
             dma((CHUNKS, nd)),
             dma((CHUNKS,)),
             dma((PIECES,)),
-            pltpu.SemaphoreType.REGULAR((2, nz)),
+            pltpu.SemaphoreType.REGULAR((3, nz)),
         ],
         compiler_params=pltpu.CompilerParams(
             collective_id=0, has_side_effects=True, vmem_limit_bytes=63 * 1024 * 1024
@@ -730,23 +768,41 @@
     )(x, g, sw, dw, count)
 
 
-def store_kernel(a_ref, b_ref, c_ref, a_out, b_out, c_out):
-    a_out[...] = a_ref[...]
-    b_out[...] = b_ref[...]
-    c_out[...] = c_ref[...]
+def store_kernel(count, *refs):
+    sources, targets, held = refs[:count], refs[count : 2 * count], refs[2 * count : 3 * count]
+    in_sem, out_sem = refs[3 * count :]
+
+    def copies(k):
+        for i in range(count):
+            step = sources[i].shape[0] // STORES
+            at = pl.ds(k * step, step)
+            yield (
+                pltpu.make_async_copy(sources[i].at[at], held[i].at[at], in_sem.at[i, k]),
+                pltpu.make_async_copy(held[i].at[at], targets[i].at[at], out_sem.at[i, k]),
+            )
+
+    for k in range(STORES):
+        for load, _ in copies(k):
+            load.start()
+    for k in range(STORES):
+        for load, store in copies(k):
+            load.wait()
+            store.start()
+    for k in range(STORES):
+        for _, store in copies(k):
+            store.wait()
 
 
 def store_results(*arrays):
-    steps = 8
-    specs = tuple(
-        pl.BlockSpec((a.shape[0] // steps, a.shape[1]), lambda i: (i, 0)) for a in arrays
-    )
+    count = len(arrays)
+    any_spec = pl.BlockSpec(memory_space=pl.ANY)
     return pl.pallas_call(
-        store_kernel,
-        grid=(steps,),
+        functools.partial(store_kernel, count),
         out_shape=tuple(jax.ShapeDtypeStruct(a.shape, a.dtype) for a in arrays),
-        in_specs=specs,
-        out_specs=specs,
+        in_specs=[any_spec] * count,
+        out_specs=(any_spec,) * count,
+        scratch_shapes=[pltpu.VMEM(a.shape, a.dtype) for a in arrays]
+        + [pltpu.SemaphoreType.DMA((count, STORES))] * 2,
         compiler_params=pltpu.CompilerParams(vmem_limit_bytes=63 * 1024 * 1024),
         name="store_results",
     )(*arrays)

time: 201 us -> 188 us (0.935)
  Pallas kernels: 200 us -> 187 us
    pallas_call x1, Pallas kernels: 188 us -> 176 us  [fused(): pl.pallas_call(functools.partial(fused_kernel, n, nd), out_shape=(jax.Sha...]
where the time goes in v2:
time: 188 us
  Pallas kernels  187 us (99%)
    pallas_call x1, Pallas kernels, fused(): pl.pallas_call(functools.partial(fused_kernel, n, nd), out_shape=(jax.Sha...  176 us
    pallas_call x1, Pallas kernels, store_results(): pl.pallas_call(functools.partial(store_kernel, count), out_shape=tuple((j...  10.2 us

profile of v2, /device:TPU:12, one launch (start us, length us, event | category | flops | bytes accessed | tf_op | source)
XLA Modules:
  0.0 187.9 jit_solution(6485535772916908542)
XLA Ops:
  1.3 176.4 %gather_backprop_reduce.1 = (f32[1024,1024]{1,0:T(8,128)}, bf16[4096,1024]{1,0:T(8,128)(2,1)}, bf16[128,4096]{1,0:T(8,128)(2,1)}) custom-call(bf16[128,4096]{1,0:T(8,128)(2,1)} %bitcast.7, bf16[128,8192]{1,0:T(8,128)(2,1)} %bitcast.6, bf16[4096,1024]{1,0:T(8,128)(2,1)} %sw_ref.1, bf16[4096,1024]{1,0:T(8,128)(2,1)} %bitcast.5, s32[1]{0:T(128)S(6)} %copy.8.count_ref), custom_call_target="tpu_custom_call" | custom-call | tf_op jit(solution)/shard_map/gather_backprop_reduce/pallas_call | solution.py:724
  177.7 10.2 %store_results.1 = (f32[1024,1024]{1,0:T(8,128)}, bf16[4096,1024]{1,0:T(8,128)(2,1)}, bf16[128,4096]{1,0:T(8,128)(2,1)}) custom-call(f32[1024,1024]{1,0:T(8,128)} %get-tuple-element.9.refs_0_, bf16[4096,1024]{1,0:T(8,128)(2,1)} %get-tuple-element.10.refs_1_, bf16[128,4096]{1,0:T(8,128)(2,1)} %get-tuple-element.11.refs_2_), custom_call_target="tpu_custom_call" | custom-call | tf_op jit(solution)/shard_map/store_results/pallas_call | solution.py:799

commit v3 on v2

--- a/solution.py
+++ b/solution.py
@@ -16,6 +16,7 @@
 HALVES = 2
 EARLY = 2
 STORES = 8
+LAG = 2
 TILE = 256
 
 
@@ -542,6 +543,7 @@
         @pl.when(j == EARLY)
         def _():
             back(farthest, turns, farthest, False)
+            flush(farthest, turns, 0, PIECES)
 
         def far_pre(chip, valid, carry):
             @pl.when(valid & (chip != farthest))
@@ -551,10 +553,6 @@
             return carry
 
         each_far(far_pre)(0)
-
-        @pl.when(j == EARLY)
-        def _():
-            flush(farthest, turns, 0, PIECES)
 
         @pl.when(j == CHUNKS - 1)
         def _():
@@ -601,7 +599,7 @@
         return rising, lax.rem(step, PIECES), (step >= 0) & (step < hops)
 
     def hop(t):
-        rising, pc, valid = turn_of(t - (z - 1))
+        rising, pc, valid = turn_of(t - LAG * (z - 1))
 
         @pl.when(valid & (z > 0) & (rising >= z))
         def _():
@@ -611,7 +609,7 @@
             def _():
                 send_up(rising, pc).start()
 
-        mirrored, pd, due = turn_of(t - (nz - 2 - z))
+        mirrored, pd, due = turn_of(t - LAG * (nz - 2 - z))
         falling = nz - 1 - mirrored
 
         @pl.when(due & (z < nz - 1) & (falling <= z))
@@ -646,7 +644,7 @@
 
         return carry
 
-    lax.fori_loop(0, max(hops + nz - 2, PIECES - 1 + spread * CHUNKS), tail_step, 0)
+    lax.fori_loop(0, max(hops + LAG * (nz - 2), PIECES - 1 + spread * CHUNKS), tail_step, 0)
 
     def in_store(pc):
         return pltpu.make_async_copy(sib.at[z, pc], in_out.at[:, depth_cols(pc)], in_sem.at[pc])

time: 188 us -> 182 us (0.968)
  Pallas kernels: 187 us -> 179 us
    pallas_call x1, Pallas kernels: 176 us -> 169 us  [fused(): pl.pallas_call(functools.partial(fused_kernel, n, nd), out_shape=(jax.Sha...]
where the time goes in v3:
time: 182 us; the launch traced here: 180 us
  Pallas kernels  179 us (98%)
    pallas_call x1, Pallas kernels, fused(): pl.pallas_call(functools.partial(fused_kernel, n, nd), out_shape=(jax.Sha...  169 us
    pallas_call x1, Pallas kernels, store_results(): pl.pallas_call(functools.partial(store_kernel, count), out_shape=tuple((j...  10.2 us

profile of v3, /device:TPU:12, one launch (start us, length us, event | category | flops | bytes accessed | tf_op | source)
XLA Modules:
  0.0 180.0 jit_solution(7713091282410590199)
XLA Ops:
  1.3 168.6 %gather_backprop_reduce.1 = (f32[1024,1024]{1,0:T(8,128)}, bf16[4096,1024]{1,0:T(8,128)(2,1)}, bf16[128,4096]{1,0:T(8,128)(2,1)}) custom-call(bf16[128,4096]{1,0:T(8,128)(2,1)} %bitcast.7, bf16[128,8192]{1,0:T(8,128)(2,1)} %bitcast.6, bf16[4096,1024]{1,0:T(8,128)(2,1)} %sw_ref.1, bf16[4096,1024]{1,0:T(8,128)(2,1)} %bitcast.5, s32[1]{0:T(128)S(6)} %copy.8.count_ref), custom_call_target="tpu_custom_call" | custom-call | tf_op jit(solution)/shard_map/gather_backprop_reduce/pallas_call | solution.py:722
  169.9 10.2 %store_results.1 = (f32[1024,1024]{1,0:T(8,128)}, bf16[4096,1024]{1,0:T(8,128)(2,1)}, bf16[128,4096]{1,0:T(8,128)(2,1)}) custom-call(f32[1024,1024]{1,0:T(8,128)} %get-tuple-element.9.refs_0_, bf16[4096,1024]{1,0:T(8,128)(2,1)} %get-tuple-element.10.refs_1_, bf16[128,4096]{1,0:T(8,128)(2,1)} %get-tuple-element.11.refs_2_), custom_call_target="tpu_custom_call" | custom-call | tf_op jit(solution)/shard_map/store_results/pallas_call | solution.py:797

commit v4 on v3

--- a/solution.py
+++ b/solution.py
@@ -16,15 +16,16 @@
 HALVES = 2
 EARLY = 2
 STORES = 8
+LIMIT = 63 * 1024 * 1024
 LAG = 2
 TILE = 256
 
 
 def fused_kernel(
     n, nd, x_ref, g_ref, sw_ref, dw_ref, count_ref, shared_out, dom_out, in_out,
-    xs, gs, weff, tb, rb, sib, chain, dxb, swb, shv,
+    xs, gs, weff, tb, rb, sib, chain, dxb,
     up_sem, down_sem, side_sem, x_sem, gsend_sem, g_sem, own_sem, sw_sem, dw_sem,
-    sib_send, sib_recv, ch_send, ch_recv, d_send, d_recv, dom_sem, out_sem, in_sem, ready,
+    sib_send, sib_recv, ch_send, ch_recv, d_send, d_recv, ready,
 ):
     me, dom = lax.axis_index("fsdp"), lax.axis_index("dom")
     nz = n // 2
@@ -73,7 +74,7 @@
         return pl.ds(pl.multiple_of((chip * 2 + core) * rows, rows), rows)
 
     def sw_load(j):
-        return pltpu.make_async_copy(sw_ref.at[:, cols(j)], swb.at[lax.rem(j, 2)], sw_sem.at[j])
+        return pltpu.make_async_copy(sw_ref.at[:, cols(j)], dom_out.at[:, cols(j)], sw_sem.at[j])
 
     def dw_load(j):
         return pltpu.make_async_copy(dw_ref.at[:, cols(j)], tb.at[j], dw_sem.at[j])
@@ -85,8 +86,7 @@
         own_sem.at[1],
     )
     for j in range(CHUNKS):
-        if j < 2:
-            sw_load(j).start()
+        sw_load(j).start()
         dw_load(j).start()
     own_x.start()
     own_g.start()
@@ -212,19 +212,13 @@
         def one(i, carry):
             at = pl.ds(pl.multiple_of(i * et, et), et)
             weff[at, cols(j)] = (
-                swb[lax.rem(j, 2), at, :].astype(F32) * tb[j, at, :].astype(F32)
+                dom_out[at, cols(j)].astype(F32) * tb[j, at, :].astype(F32)
             ).astype(BF16)
             return carry
 
         lax.fori_loop(0, depth // et, one, 0)
 
-        @pl.when(j + 2 < CHUNKS)
-        def _():
-            sw_load(j + 2).start()
-
     each_chunk(make_weff)
-    for j in range(2):
-        sw_load(j).start()
     own_x.wait()
     own_g.wait()
 
@@ -481,23 +475,7 @@
             total = total + rb[at, j, here, :].astype(F32)
         return total
 
-    def dom_store(j, m):
-        return pltpu.make_async_copy(
-            swb.at[lax.rem(j, 2), block_rows(m)],
-            dom_out.at[block_rows(m), cols(j)],
-            dom_sem.at[j, m],
-        )
-
     def weight_chunk(j):
-        sw_load(j).wait()
-
-        @pl.when((j >= 1) & (j + 1 < CHUNKS))
-        def _():
-            for m in range(nd):
-                dom_store(j - 1, m).wait()
-            sw_load(j + 1).start()
-
-        slot = lax.rem(j, 2)
         for m in order:
             at = block_rows(m)
             scaled = scale * lax.dot_general(
@@ -507,8 +485,7 @@
             for q in range(pieces):
                 if sent_at(m, q % parts) == 0:
                     d_copy(j, m, q).start()
-            swb[slot, at, :] = (scaled * swb[slot, at, :].astype(F32)).astype(BF16)
-            dom_store(j, m).start()
+            dom_out[at, cols(j)] = (scaled * dom_out[at, cols(j)].astype(F32)).astype(BF16)
 
     def wait_far_x(chip, valid, carry):
         @pl.when(valid)
@@ -629,9 +606,6 @@
                         tb[j, tile_rows(m, q), :] = total
                         d_copy(j, m, q).start()
 
-    def shared_store(j):
-        return pltpu.make_async_copy(shv.at[j], shared_out.at[:, cols(j)], out_sem.at[j])
-
     spread = PIECES // 2
 
     def tail_step(t, carry):
@@ -646,21 +620,14 @@
 
     lax.fori_loop(0, max(hops + LAG * (nz - 2), PIECES - 1 + spread * CHUNKS), tail_step, 0)
 
-    def in_store(pc):
-        return pltpu.make_async_copy(sib.at[z, pc], in_out.at[:, depth_cols(pc)], in_sem.at[pc])
-
-    each_piece(lambda pc: in_store(pc).start())
+    for pc in range(PIECES):
+        in_out[:, pc * pw : (pc + 1) * pw] = sib[z, pc]
 
     def final(j):
         for q in range(pieces):
-            shv[j, pl.ds(q * tile, tile), :] = arrived(j, 0, q, bits)
-        shared_store(j).start()
+            shared_out[pl.ds(q * tile, tile), cols(j)] = arrived(j, 0, q, bits)
 
     each_chunk(final)
-
-    for j in range(max(0, CHUNKS - 2), CHUNKS):
-        for m in range(nd):
-            dom_store(j, m).wait()
 
     def drain_chip(chip, carry):
         for h in range(HALVES):
@@ -700,10 +667,8 @@
         for m in range(1, nd):
             for q in range(pieces):
                 d_copy(j, m, q).wait_send()
-        shared_store(j).wait()
 
     each_chunk(drain_d)
-    each_piece(lambda pc: in_store(pc).wait())
 
 
 def fused(n, nd, x, g, sw, dw, count):
@@ -716,18 +681,19 @@
     tile = min(TILE, block // min(2, bits))
     pieces = block // tile
     cw, pw = width // CHUNKS, depth // PIECES
+    kept = block * width * 4 + depth * width * 2 + rows * depth * 2
     any_spec = pl.BlockSpec(memory_space=pl.ANY)
     dma = pltpu.SemaphoreType.DMA
     vmem = pltpu.VMEM
     return pl.pallas_call(
         functools.partial(fused_kernel, n, nd),
         out_shape=(
-            jax.ShapeDtypeStruct((block, width), F32),
-            jax.ShapeDtypeStruct((depth, width), BF16),
-            jax.ShapeDtypeStruct((rows, depth), BF16),
+            vmem((block, width), F32),
+            vmem((depth, width), BF16),
+            vmem((rows, depth), BF16),
         ),
         in_specs=[any_spec] * 4 + [pl.BlockSpec(memory_space=pltpu.SMEM)],
-        out_specs=(any_spec,) * 3,
+        out_specs=(pl.BlockSpec(memory_space=vmem),) * 3,
         scratch_shapes=[
             vmem((total, depth), BF16),
             vmem((total, width), BF16),
@@ -737,8 +703,6 @@
             vmem((nz, PIECES, rows, pw), BF16),
             vmem((nz + 1, PIECES, rows, pw), BF16),
             vmem((2, PIECES, 2 * rows, pw), BF16),
-            vmem((2, depth, cw), BF16),
-            vmem((CHUNKS, block, cw), F32),
             dma((nz, HALVES)),
             dma((nz, HALVES)),
             dma((nz, HALVES)),
@@ -754,54 +718,38 @@
             dma((nz + 1, PIECES)),
             dma((nd - 1, CHUNKS, pieces)),
             dma((nd - 1, CHUNKS, pieces)),
-            dma((CHUNKS, nd)),
-            dma((CHUNKS,)),
-            dma((PIECES,)),
             pltpu.SemaphoreType.REGULAR((3, nz)),
         ],
         compiler_params=pltpu.CompilerParams(
-            collective_id=0, has_side_effects=True, vmem_limit_bytes=63 * 1024 * 1024
+            collective_id=0, has_side_effects=True, vmem_limit_bytes=LIMIT - kept
         ),
         name="gather_backprop_reduce",
     )(x, g, sw, dw, count)
 
 
 def store_kernel(count, *refs):
-    sources, targets, held = refs[:count], refs[count : 2 * count], refs[2 * count : 3 * count]
-    in_sem, out_sem = refs[3 * count :]
-
-    def copies(k):
-        for i in range(count):
-            step = sources[i].shape[0] // STORES
+    sources, targets, sem = refs[:count], refs[count : 2 * count], refs[2 * count]
+    copies = []
+    for i in range(count):
+        step = sources[i].shape[0] // STORES
+        for k in range(STORES):
             at = pl.ds(k * step, step)
-            yield (
-                pltpu.make_async_copy(sources[i].at[at], held[i].at[at], in_sem.at[i, k]),
-                pltpu.make_async_copy(held[i].at[at], targets[i].at[at], out_sem.at[i, k]),
-            )
-
-    for k in range(STORES):
-        for load, _ in copies(k):
-            load.start()
-    for k in range(STORES):
-        for load, store in copies(k):
-            load.wait()
-            store.start()
-    for k in range(STORES):
-        for _, store in copies(k):
-            store.wait()
+            copies.append(pltpu.make_async_copy(sources[i].at[at], targets[i].at[at], sem.at[i, k]))
+    for copy in copies:
+        copy.start()
+    for copy in copies:
+        copy.wait()
 
 
 def store_results(*arrays):
     count = len(arrays)
-    any_spec = pl.BlockSpec(memory_space=pl.ANY)
     return pl.pallas_call(
         functools.partial(store_kernel, count),
         out_shape=tuple(jax.ShapeDtypeStruct(a.shape, a.dtype) for a in arrays),
-        in_specs=[any_spec] * count,
-        out_specs=(any_spec,) * count,
-        scratch_shapes=[pltpu.VMEM(a.shape, a.dtype) for a in arrays]
-        + [pltpu.SemaphoreType.DMA((count, STORES))] * 2,
-        compiler_params=pltpu.CompilerParams(vmem_limit_bytes=63 * 1024 * 1024),
+        in_specs=[pl.BlockSpec(memory_space=pltpu.VMEM)] * count,
+        out_specs=(pl.BlockSpec(memory_space=pl.ANY),) * count,
+        scratch_shapes=[pltpu.SemaphoreType.DMA((count, STORES))],
+        compiler_params=pltpu.CompilerParams(vmem_limit_bytes=16 * 1024 * 1024),
         name="store_results",
     )(*arrays)
 
@@ -813,6 +761,7 @@
         results = fused(
             n, nd, inputs[0], cotangent[0], shared_weight, domain_weight[0], row_counts
         )
+        results = [pltpu.with_memory_space_constraint(a, pltpu.VMEM) for a in results]
         shared_grad, domain_grad, input_grad = store_results(*results)
         return (shared_grad, domain_grad[None], input_grad[None])
 

time: 182 us -> 177 us (0.973)
  Pallas kernels: 179 us -> 173 us
    pallas_call x1, Pallas kernels: 10.2 us -> 5.05 us  [store_results(): pl.pallas_call(functools.partial(store_kernel, count), out_shape=tuple((j...]
where the time goes in v4:
time: 177 us; the launch traced here: 175 us
  Pallas kernels  173 us (98%)
    pallas_call x1, Pallas kernels, fused(): pl.pallas_call(functools.partial(fused_kernel, n, nd), out_shape=(vmem((b...  168 us
    pallas_call x1, Pallas kernels, store_results(): pl.pallas_call(functools.partial(store_kernel, count), out_shape=tuple((j...  5.05 us

profile of v4, /device:TPU:12, one launch (start us, length us, event | category | flops | bytes accessed | tf_op | source)
XLA Modules:
  0.0 174.6 jit_solution(17637012184432455243)
XLA Ops:
  1.3 168.3 %gather_backprop_reduce.1 = (f32[1024,1024]{1,0:T(8,128)S(1)}, bf16[4096,1024]{1,0:T(8,128)(2,1)S(1)}, bf16[128,4096]{1,0:T(8,128)(2,1)S(1)}) custom-call(bf16[128,4096]{1,0:T(8,128)(2,1)} %bitcast.7, bf16[128,8192]{1,0:T(8,128)(2,1)} %bitcast.6, bf16[4096,1024]{1,0:T(8,128)(2,1)} %sw_ref.1, bf16[4096,1024]{1,0:T(8,128)(2,1)} %bitcast.5, s32[1]{0:T(128)S(6)} %copy.8.count_ref), custom_call_target="tpu_custom_call" | custom-call | tf_op jit(solution)/shard_map/gather_backprop_reduce/pallas_call | solution.py:688
  169.6 5.0 %store_results.1 = (f32[1024,1024]{1,0:T(8,128)}, bf16[4096,1024]{1,0:T(8,128)(2,1)}, bf16[128,4096]{1,0:T(8,128)(2,1)}) custom-call(f32[1024,1024]{1,0:T(8,128)S(1)} %get-tuple-element.9.refs_0_, bf16[4096,1024]{1,0:T(8,128)(2,1)S(1)} %get-tuple-element.10.refs_1_, bf16[128,4096]{1,0:T(8,128)(2,1)S(1)} %get-tuple-element.11.refs_2_), custom_call_target="tpu_custom_call" | custom-call | tf_op jit(solution)/shard_map/store_results/pallas_call | solution.py:746

commit v5 on v4

--- a/solution.py
+++ b/solution.py
@@ -244,15 +244,15 @@
         ).wait_recv()
 
     def pre(chip, j):
-        wait_g(chip, 1 - c, j)
-
-        @pl.when(chip != z)
-        def _():
-            wait_g(chip, c, j)
-
         here = chip_rows(chip)
         preact = jnp.dot(xs[here, :], weff[:, cols(j)], preferred_element_type=F32)
         sigma = jax.nn.sigmoid(preact)
+        wait_g(chip, 1 - c, j)
+
+        @pl.when(chip != z)
+        def _():
+            wait_g(chip, c, j)
+
         position = chip * (2 * rows) + lax.broadcasted_iota(jnp.int32, preact.shape, 0)
         slope = gs[here, cols(j)].astype(F32) * sigma * (1.0 + preact * (1.0 - sigma))
         gs[here, cols(j)] = jnp.where(position < count, slope, 0.0).astype(BF16)

time: 177 us -> 177 us (level)
  no operation moved by 1% of the time
where the time goes in v5:
time: 177 us; the launch traced here: 175 us
  Pallas kernels  174 us (98%)
    pallas_call x1, Pallas kernels, fused(): pl.pallas_call(functools.partial(fused_kernel, n, nd), out_shape=(vmem((b...  169 us
    pallas_call x1, Pallas kernels, store_results(): pl.pallas_call(functools.partial(store_kernel, count), out_shape=tuple((j...  5.05 us

profile of v5, /device:TPU:12, one launch (start us, length us, event | category | flops | bytes accessed | tf_op | source)
XLA Modules:
  0.0 175.1 jit_solution(1855924871324867631)
XLA Ops:
  1.3 168.6 %gather_backprop_reduce.1 = (f32[1024,1024]{1,0:T(8,128)S(1)}, bf16[4096,1024]{1,0:T(8,128)(2,1)S(1)}, bf16[128,4096]{1,0:T(8,128)(2,1)S(1)}) custom-call(bf16[128,4096]{1,0:T(8,128)(2,1)} %bitcast.7, bf16[128,8192]{1,0:T(8,128)(2,1)} %bitcast.6, bf16[4096,1024]{1,0:T(8,128)(2,1)} %sw_ref.1, bf16[4096,1024]{1,0:T(8,128)(2,1)} %bitcast.5, s32[1]{0:T(128)S(6)} %copy.8.count_ref), custom_call_target="tpu_custom_call" | custom-call | tf_op jit(solution)/shard_map/gather_backprop_reduce/pallas_call | solution.py:688
  169.9 5.0 %store_results.1 = (f32[1024,1024]{1,0:T(8,128)}, bf16[4096,1024]{1,0:T(8,128)(2,1)}, bf16[128,4096]{1,0:T(8,128)(2,1)}) custom-call(f32[1024,1024]{1,0:T(8,128)S(1)} %get-tuple-element.9.refs_0_, bf16[4096,1024]{1,0:T(8,128)(2,1)S(1)} %get-tuple-element.10.refs_1_, bf16[128,4096]{1,0:T(8,128)(2,1)S(1)} %get-tuple-element.11.refs_2_), custom_call_target="tpu_custom_call" | custom-call | tf_op jit(solution)/shard_map/store_results/pallas_call | solution.py:746
